TPU v7x, 128 devices: a whole 4x4x4 slice. The times are simulated.
128 devices in a mesh: gx: 16 (over z_lo, x, core), gy: 8 (over y, z_hi).
Axes of the slice: x: 4, y: 4, z: 4 (z_hi: 2, z_lo: 2; z = z_hi * 2 + z_lo), core: 2. Of those that a mesh axis runs over, the one named last changes fastest.
Arguments:
- features: bfloat16 [64, 128, 64, 128], P(None, 'gx', 'gy'), may hold values from -6 to 6
- cotangent: bfloat16 [64, 128, 64, 128], P(None, 'gx', 'gy'), may hold values from -6 to 6
- block_mask: int32 [16, 8, 16], P('gx', 'gy'), may hold values from 0 to 1, as said below
- kernel_one: bfloat16 [3, 3, 3, 64, 64], replicated, may hold values from -0.15625 to 0.15625
- kernel_two: bfloat16 [3, 3, 3, 64, 64], replicated, may hold values from -0.15625 to 0.15625
Outputs:
- grad_features: bfloat16 [64, 128, 64, 128], P(None, 'gx', 'gy')
- grad_one: float32 [3, 3, 3, 64, 64], replicated
- grad_two: float32 [3, 3, 3, 64, 64], replicated
Inputs may be any that keep to these rules, and one draw needn't show every extreme that they name: `block_mask`: 1 marks an active block of 8 x 8 x 8 cells, 0 an empty one.
All inputs are finite; a program needn't handle non-finite values.
Results may differ from a plain program's by a relative error of at most 0.0032.
Values may be sent and summed in bfloat16 or wider, within the bound.
No kernel may reach another device: no remote copies, remote signals or barrier semaphores. Data moves between devices by JAX's collectives and lax.ppermute only.
A program may use at most 192 MiB of HBM per device.

v0:
```python
import math
import jax
import jax.numpy as jnp
from jax import lax
from jax.sharding import PartitionSpec as P

BS = 8


def padded_2(cells, sides, width):
    for axis, dim in sides:
        count = lax.axis_size(axis)
        ends = count - 1
        head = lax.slice_in_dim(cells, 0, width, axis=dim)
        tail = lax.slice_in_dim(cells, cells.shape[dim] - width, cells.shape[dim], axis=dim)
        cells = jnp.concatenate(
            [
                lax.ppermute(tail, axis, [(i, (i + 1) % count) for i in range(ends)]),
                cells,
                lax.ppermute(head, axis, [((i + 1) % count, i) for i in range(ends)]),
            ],
            axis=dim,
        )
    return cells


def upsample(block_mask):
    nbx, nby, nbz = block_mask.shape
    wide = jnp.broadcast_to(block_mask[:, None, :, None, :, None], (nbx, BS, nby, BS, nbz, BS))
    return wide.reshape(nbx * BS, nby * BS, nbz * BS)


def flip_kernel(kernel):
    return jnp.transpose(jnp.flip(kernel, (0, 1, 2)), (0, 1, 2, 4, 3))


def silu_slope(value):
    sig = jax.nn.sigmoid(value)
    return sig * (1.0 + value * (1.0 - sig))


def stack_depth(source):
    depth = source.shape[-1]
    padded = jnp.pad(source, ((0, 0), (0, 0), (0, 0), (1, 1)))
    return jnp.concatenate(
        [padded[..., 0:depth], padded[..., 1 : depth + 1], padded[..., 2 : depth + 2]], 0
    )


def stack_reverse(source):
    depth = source.shape[-1]
    padded = jnp.pad(source, ((0, 0), (0, 0), (0, 0), (1, 1)))
    return jnp.concatenate(
        [padded[..., 2 : depth + 2], padded[..., 1 : depth + 1], padded[..., 0:depth]], 0
    )


def conv_pad(source, kernel, size_x, size_y):
    stacked = stack_depth(source)
    folded = kernel.reshape(3, 3, 3 * kernel.shape[3], kernel.shape[4])
    total = None
    for row_off in range(3):
        for col_off in range(3):
            window = stacked[:, row_off : row_off + size_x, col_off : col_off + size_y]
            term = jnp.einsum(
                "co,cxyz->oxyz",
                folded[row_off, col_off],
                window,
                preferred_element_type=jnp.float32,
            )
            total = term if total is None else total + term
    return total


def grad_forward(source, grad, size_x, size_y):
    stacked = stack_depth(source)
    pieces = []
    for row_off in range(3):
        for col_off in range(3):
            window = stacked[:, row_off : row_off + size_x, col_off : col_off + size_y]
            pieces.append(
                jnp.einsum("cxyz,oxyz->co", window, grad, preferred_element_type=jnp.float32)
            )
    return jnp.stack(pieces, 0).reshape(3, 3, 3, source.shape[0], grad.shape[0])


def grad_backward(activ, grad_pad, size_x, size_y):
    stacked = stack_reverse(grad_pad)
    pieces = []
    for row_off in range(3):
        for col_off in range(3):
            start_x = 2 - row_off
            start_y = 2 - col_off
            window = stacked[:, start_x : start_x + size_x, start_y : start_y + size_y]
            block = jnp.einsum("cxyz,kxyz->ck", activ, window, preferred_element_type=jnp.float32)
            block = block.reshape(activ.shape[0], 3, grad_pad.shape[0])
            pieces.append(jnp.transpose(block, (1, 0, 2)))
    return jnp.stack(pieces, 0).reshape(3, 3, 3, activ.shape[0], grad_pad.shape[0])


def shards(features, cotangent, block_mask, kernel_one, kernel_two):
    chans, tile_x, tile_y, tile_z = features.shape
    cell = upsample(block_mask).astype(jnp.bfloat16)[None]
    cell_f = cell.astype(jnp.float32)
    masked_in = features * cell
    masked_grad = cotangent * cell
    flip_one = flip_kernel(kernel_one)
    flip_two = flip_kernel(kernel_two)
    cells_all = tile_x * tile_y * tile_z * lax.axis_size("gx") * lax.axis_size("gy")
    scale = 1.0 / math.sqrt(cells_all)
    in_pad, grad_pad = (
        padded_2(masked_in, (("gx", 1), ("gy", 2)), 1),
        padded_2(masked_grad, (("gx", 1), ("gy", 2)), 1),
    )
    pre_act = conv_pad(in_pad, kernel_one, tile_x, tile_y)
    activ = (cell_f * jax.nn.silu(pre_act)).astype(jnp.bfloat16)
    partial_two = grad_backward(activ, grad_pad, tile_x, tile_y)
    summed_two = partial_two
    act_grad = conv_pad(grad_pad, flip_two, tile_x, tile_y)
    pre_grad = (cell_f * silu_slope(pre_act) * act_grad).astype(jnp.bfloat16)
    hidden_pad = padded_2(pre_grad, (("gx", 1), ("gy", 2)), 1)
    partial_one = grad_forward(in_pad, pre_grad, tile_x, tile_y)
    branch = conv_pad(hidden_pad, flip_one, tile_x, tile_y)
    grad_features = (cell_f * (cotangent.astype(jnp.float32) + branch)).astype(jnp.bfloat16)
    summed_one, summed_two = lax.psum((partial_one, summed_two), ("gx", "gy"))
    return (grad_features, summed_one * scale, summed_two * scale)


def solution(mesh):
    placed = (P(None, "gx", "gy", None), P(None, "gx", "gy", None), P("gx", "gy", None), P(), P())
    return jax.shard_map(
        shards,
        mesh=mesh,
        in_specs=placed,
        out_specs=(P(None, "gx", "gy", None), P(), P()),
        check_vma=False,
    )
```

profile of v0, /device:TPU:1, one launch (start us, length us, event | category | flops | bytes accessed | tf_op | source)
XLA Modules:
  0.0 286.3 jit_solution(6869526273240850333)
XLA Ops:
  8.1 3.3 %copy_multiply_fusion.1 = (bf16[64,8,8,128]{3,0,2,1:T(8,128)(2,1)S(1)}, bf16[64,8,8,128]{3,0,2,1:T(8,128)(2,1)S(1)}) fusion(bf16[64,8,8,128]{3,2,1,0:T(8,128)(2,1)} %param.6, bf16[128]{0:T(256)(128)(2,1)S(1)} %convert_element_type.40, bf16[64,8,8,128]{3,2,1,0:T(8,128)(2,1)} %param.5), kind=kLoop, calls=%fused_computation.141 | loop fusion | flops 1048576 | bytes 4194560 | tf_op jit(solution)/shard_map/mul | solution.py:106
  11.5 4.5 %collective-permute-start = (bf16[64,1,8,128]{3,0,2,1:T(8,128)(2,1)S(1)}, bf16[64,1,8,128]{3,0,2,1:T(8,128)(2,1)S(1)}, u32[]{:S(2)}, u32[]{:S(2)}) collective-permute-start(bf16[64,1,8,128]{3,0,2,1:T(8,128)(2,1)S(1)} %get-tuple-element.29), channel_id=1, source_target_pairs={{0,8},{8,16},{16,24},{24,32},{32,40},{40,48},{48,56},{56,64},{64,7... | collective-permute-start | bytes 393224 | tf_op jit(solution)/shard_map/ppermute | solution.py:18
  16.0 1.9 collective-permute-start.1
  18.6 3.8 %collective-permute-start.4 = (bf16[64,1,8,128]{3,0,2,1:T(8,128)(2,1)}, bf16[64,1,8,128]{3,0,2,1:T(8,128)(2,1)S(1)}, u32[]{:S(2)}, u32[]{:S(2)}) collective-permute-start(bf16[64,1,8,128]{3,0,2,1:T(8,128)(2,1)} %get-tuple-element.27), channel_id=1, source_target_pairs={{0,8},{8,16},{16,24},{24,32},{32,40},{40,48},{48,56},{56,64},{64,7... | collective-permute-start | bytes 393224 | tf_op jit(solution)/shard_map/ppermute | solution.py:18
  22.4 1.9 collective-permute-start.5
  25.2 6.2 %collective-permute-start.2 = (bf16[64,10,1,128]{3,0,2,1:T(8,128)(2,1)}, bf16[64,10,1,128]{3,0,2,1:T(8,128)(2,1)}, u32[]{:S(2)}, u32[]{:S(2)}) collective-permute-start(bf16[64,10,1,128]{3,0,2,1:T(8,128)(2,1)} %get-tuple-element.23), channel_id=1, source_target_pairs={{0,1},{1,2},{2,3},{3,4},{4,5},{5,6},{6,7},{8,9},{9,10},{10,11},{11... | collective-permute-start | bytes 491528 | tf_op jit(solution)/shard_map/ppermute | solution.py:18
  35.9 5.5 %collective-permute-start.6 = (bf16[64,10,1,128]{3,0,2,1:T(8,128)(2,1)S(1)}, bf16[64,10,1,128]{3,0,2,1:T(8,128)(2,1)S(1)}, u32[]{:S(2)}, u32[]{:S(2)}) collective-permute-start(bf16[64,10,1,128]{3,0,2,1:T(8,128)(2,1)S(1)} %get-tuple-element.21), channel_id=1, source_target_pairs={{0,1},{1,2},{2,3},{3,4},{4,5},{5,6},{6,7},{8,9},{9,10},{10,11},{11... | collective-permute-start | bytes 491528 | tf_op jit(solution)/shard_map/ppermute | solution.py:18
  41.4 1.8 collective-permute-start.7
  43.2 4.0 %fusion.15 = bf16[64,10,10,130]{3,0,2,1:T(8,128)(2,1)S(1)} fusion(bf16[64,10,1,128]{3,0,2,1:T(8,128)(2,1)} %collective-permute-done.3, bf16[64,10,1,128]{3,0,2,1:T(8,128)(2,1)} %collective-permute-done.2, bf16[64,1,8,128]{3,0,2,1:T(8,128)(2,1)} %copy-done.6, bf16[64,8,8,128]{3,0,2,1:T(8,128)(2,1)S(1)} %get-tuple-element.32, bf16[64,1,8,128]{3,0,2,1:T(8,128)(2,1)} %copy-done.4), kind=kLoop, calls=%fused_computation.24 | loop fusion | flops 14976000 | bytes 3302400 | tf_op jit(solution)/shard_map/concatenate | solution.py:16
  48.2 4.9 %pad_maximum_fusion = bf16[192,10,10,128]{3,0,2,1:T(8,128)(2,1)S(1)} fusion(bf16[64,10,10,128]{3,0,2,1:T(8,128)(2,1)S(1)} %get-tuple-element.18, bf16[64,10,1,128]{3,0,2,1:T(8,128)(2,1)} %collective-permute-done.3, bf16[64,1,8,128]{3,0,2,1:T(8,128)(2,1)S(1)} %copy-done.7, bf16[64,8,8,128]{3,0,2,1:T(8,128)(2,1)S(1)} %get-tuple-element.32, ...), kind=kLoop, calls=%fused_computation.3 | loop fusion | flops 34406400 | bytes 9830400 | tf_op jit(solution)/shard_map/concatenate | solution.py:45
  59.1 3.9 %fusion.19 = bf16[64,10,10,130]{3,0,2,1:T(8,128)(2,1)S(1)} fusion(bf16[64,10,1,128]{3,0,2,1:T(8,128)(2,1)S(1)} %collective-permute-done.7, bf16[64,10,1,128]{3,0,2,1:T(8,128)(2,1)S(1)} %collective-permute-done.6, bf16[64,1,8,128]{3,0,2,1:T(8,128)(2,1)} %collective-permute-done.5, bf16[64,8,8,128]{3,0,2,1:T(8,128)(2,1)S(1)} %get-tuple-element.31, ...), kind=kLoop, calls=%fused_computation.28 | loop fusion | flops 14976000 | bytes 3302400 | tf_op jit(solution)/shard_map/concatenate | solution.py:16
  63.0 2.1 fusion.123
  66.9 5.4 %pad_maximum_fusion.4 = (bf16[192,10,10,128]{3,0,2,1:T(8,128)(2,1)S(1)}, bf16[192,10,10,128]{3,0,2,1:T(8,128)(2,1)S(1)}) fusion(bf16[64,10,10,128]{3,0,2,1:T(8,128)(2,1)S(1)} %get-tuple-element.15, bf16[64,10,10,128]{3,0,2,1:T(8,128)(2,1)} %get-tuple-element.16, bf16[64,10,1,128]{3,0,2,1:T(8,128)(2,1)S(1)} %collective-permute-done.7, ...), kind=kLoop, calls=%fused_computation.7 | loop fusion | flops 46694400 | bytes 14745600 | tf_op jit(solution)/shard_map/concatenate | solution.py:53
  86.8 2.1 fusion.76
  88.9 3.5 %fusion.98 = bf16[64,8,8,128]{3,0,2,1:T(8,128)(2,1)S(1)} fusion(f32[8,8,128,64]{2,3,1,0:T(8,128)S(1)} %get-tuple-element.34, f32[8,8,128,64]{2,3,1,0:T(8,128)S(1)} %fusion.62, f32[8,8,128,64]{2,3,1,0:T(8,128)S(1)} %fusion.64, f32[8,8,128,64]{2,3,1,0:T(8,128)S(1)} %fusion.66, f32[8,8,128,64]{2,3,1,0:T(8,128)S(1)} %fusion.68, ...), kind=kOutput, calls=%fused_computation.109 | convolution fusion | flops 210763776 | bytes 23118336 | tf_op jit(solution)/shard_map/co,cxyz->oxyz/dot_general | solution.py:65
  93.6 4.5 %collective-permute-start.8 = (bf16[64,1,8,128]{3,0,2,1:T(8,128)(2,1)S(1)}, bf16[64,1,8,128]{3,0,2,1:T(8,128)(2,1)S(1)}, u32[]{:S(2)}, u32[]{:S(2)}) collective-permute-start(bf16[64,1,8,128]{3,0,2,1:T(8,128)(2,1)S(1)} %get-tuple-element.25), channel_id=1, source_target_pairs={{0,8},{8,16},{16,24},{24,32},{32,40},{40,48},{48,56},{56,64},{64,7... | collective-permute-start | bytes 393224 | tf_op jit(solution)/shard_map/ppermute | solution.py:18
  98.1 1.9 collective-permute-start.9
  109.1 5.8 %collective-permute-start.10 = (bf16[64,10,1,128]{3,0,2,1:T(8,128)(2,1)S(1)}, bf16[64,10,1,128]{3,0,2,1:T(8,128)(2,1)S(1)}, u32[]{:S(2)}, u32[]{:S(2)}) collective-permute-start(bf16[64,10,1,128]{3,0,2,1:T(8,128)(2,1)S(1)} %get-tuple-element.19), channel_id=1, source_target_pairs={{0,1},{1,2},{2,3},{3,4},{4,5},{5,6},{6,7},{8,9},{9,10},{10,11},{11... | collective-permute-start | bytes 491528 | tf_op jit(solution)/shard_map/ppermute | solution.py:18
  118.9 3.6 %collective-permute-done.11 = bf16[64,10,1,128]{3,0,2,1:T(8,128)(2,1)S(1)} collective-permute-done((bf16[64,10,1,128]{3,0,2,1:T(8,128)(2,1)S(1)}, bf16[64,10,1,128]{3,0,2,1:T(8,128)(2,1)S(1)}, u32[]{:S(2)}, u32[]{:S(2)}) %collective-permute-start.11) | collective-permute-done | bytes 163872 | tf_op jit(solution)/shard_map/ppermute | solution.py:20
  122.5 3.1 %select_maximum_fusion = bf16[64,10,10,130]{3,0,2,1:T(8,128)(2,1)S(1)} fusion(bf16[64,10,1,128]{3,0,2,1:T(8,128)(2,1)S(1)} %collective-permute-done.11, bf16[64,10,1,128]{3,0,2,1:T(8,128)(2,1)S(1)} %collective-permute-done.10, bf16[64,1,8,128]{3,0,2,1:T(8,128)(2,1)S(1)} %collective-permute-done.9, bf16[64,8,8,128]{3,0,2,1:T(8,128)(2,1)S(1)} %fusion.98, ...), kind=kLoop, calls=%fused_computation.8 | loop fusion | flops 14976000 | bytes 3302400 | tf_op jit(solution)/shard_map/concatenate | solution.py:16
  126.5 4.3 %pad_maximum_fusion.3 = bf16[192,10,10,128]{3,0,2,1:T(8,128)(2,1)S(1)} fusion(bf16[64,10,10,128]{3,0,2,1:T(8,128)(2,1)S(1)} %get-tuple-element.14, bf16[64,10,1,128]{3,0,2,1:T(8,128)(2,1)S(1)} %collective-permute-done.11, bf16[64,1,8,128]{3,0,2,1:T(8,128)(2,1)S(1)} %collective-permute-done.9, bf16[64,8,8,128]{3,0,2,1:T(8,128)(2,1)S(1)} %fusion.98, ...), kind=kLoop, calls=%fused_computation.6 | loop fusion | flops 34406400 | bytes 9830400 | tf_op jit(solution)/shard_map/concatenate | solution.py:45
  137.2 2.2 fusion.97
  141.1 135.2 %all-reduce.6.cloned.1.call-done = (f32[3,3,3,64,64]{4,3,2,1,0:T(8,128)}, f32[3,3,3,64,64]{4,3,2,1,0:T(8,128)}) async-done(((f32[3,3,3,64,64]{4,3,2,1,0:T(8,128)}, f32[3,3,3,64,64]{4,3,2,1,0:T(8,128)}), (f32[3,3,3,64,64]{4,3,2,1,0:T(8,128)}, f32[3,3,3,64,64]{4,3,2,1,0:T(8,128)})) %all-reduce.6.cloned.1.call-update) | async-done | bytes 884752 | tf_op jit(solution)/shard_map/psum | solution.py:125
  276.3 2.9 %broadcast_multiply_fusion = (f32[3,3,3,64,64]{4,3,2,1,0:T(8,128)}, f32[3,3,3,64,64]{4,3,2,1,0:T(8,128)}) fusion(f32[3,3,3,64,64]{4,3,2,1,0:T(8,128)} %get-tuple-element.10, f32[3,3,3,64,64]{4,3,2,1,0:T(8,128)} %get-tuple-element.9), kind=kLoop, calls=%fused_computation.142 | loop fusion | flops 221184 | bytes 1769472 | tf_op jit(solution)/shard_map/mul | solution.py:126
  (111 shorter events, 53.1 us)
Async XLA Ops:
  7.2 17.2 %copy-start.8 = (bf16[3,3,3,64,64]{4,3,2,1,0:T(8,128)(2,1)S(1)}, bf16[3,3,3,64,64]{4,3,2,1,0:T(8,128)(2,1)}, u32[]{:S(2)}) copy-start(bf16[3,3,3,64,64]{4,3,2,1,0:T(8,128)(2,1)} %param.9) | copy-start | bytes 663556
  7.2 269.2 %all-reduce.6.cloned.1.call-start = ((), (), s32[]{:S(2)}) async-start(), calls=%async_computation | async-start | bytes 3538944 | tf_op jit(solution)/shard_map/psum | solution.py:125
  8.1 10.5 %copy-start.11 = (bf16[128]{0:T(256)(128)(2,1)}, bf16[128]{0:T(256)(128)(2,1)S(1)}, u32[]{:S(2)}) copy-start(bf16[128]{0:T(256)(128)(2,1)S(1)} %convert_element_type.40) | copy-start | bytes 772
  8.1 24.5 %copy-start.1 = (bf16[3,3,3,64,64]{4,3,2,1,0:T(8,128)(2,1)S(1)}, bf16[3,3,3,64,64]{4,3,2,1,0:T(8,128)(2,1)}, u32[]{:S(2)}) copy-start(bf16[3,3,3,64,64]{4,3,2,1,0:T(8,128)(2,1)} %param.8) | copy-start | bytes 663556
  11.5 12.9 %collective-permute-start = (bf16[64,1,8,128]{3,0,2,1:T(8,128)(2,1)S(1)}, bf16[64,1,8,128]{3,0,2,1:T(8,128)(2,1)S(1)}, u32[]{:S(2)}, u32[]{:S(2)}) collective-permute-start(bf16[64,1,8,128]{3,0,2,1:T(8,128)(2,1)S(1)} %get-tuple-element.29), channel_id=1, source_target_pairs={{0,8},{8,16},{16,24},{24,32},{32,40},{40,48},{48,56},{56,64},{64,7... | collective-permute-start | bytes 393224 | tf_op jit(solution)/shard_map/ppermute | solution.py:18
  16.0 8.4 %collective-permute-start.1 = (bf16[64,1,8,128]{3,0,2,1:T(8,128)(2,1)S(1)}, bf16[64,1,8,128]{3,0,2,1:T(8,128)(2,1)S(1)}, u32[]{:S(2)}, u32[]{:S(2)}) collective-permute-start(bf16[64,1,8,128]{3,0,2,1:T(8,128)(2,1)S(1)} %get-tuple-element.30), channel_id=1, source_target_pairs={{8,0},{16,8},{24,16},{32,24},{40,32},{48,40},{56,48},{64,56},{72,6... | collective-permute-start | bytes 393224 | tf_op jit(solution)/shard_map/ppermute | solution.py:20
  18.6 14.1 %copy-start.12 = (bf16[128]{0:T(256)(128)(2,1)S(1)}, bf16[128]{0:T(256)(128)(2,1)}, u32[]{:S(2)}) copy-start(bf16[128]{0:T(256)(128)(2,1)} %copy-done.11) | copy-start | bytes 772
  18.6 16.5 %collective-permute-start.4 = (bf16[64,1,8,128]{3,0,2,1:T(8,128)(2,1)}, bf16[64,1,8,128]{3,0,2,1:T(8,128)(2,1)S(1)}, u32[]{:S(2)}, u32[]{:S(2)}) collective-permute-start(bf16[64,1,8,128]{3,0,2,1:T(8,128)(2,1)} %get-tuple-element.27), channel_id=1, source_target_pairs={{0,8},{8,16},{16,24},{24,32},{32,40},{40,48},{48,56},{56,64},{64,7... | collective-permute-start | bytes 393224 | tf_op jit(solution)/shard_map/ppermute | solution.py:18
  22.4 12.7 %collective-permute-start.5 = (bf16[64,1,8,128]{3,0,2,1:T(8,128)(2,1)}, bf16[64,1,8,128]{3,0,2,1:T(8,128)(2,1)}, u32[]{:S(2)}, u32[]{:S(2)}) collective-permute-start(bf16[64,1,8,128]{3,0,2,1:T(8,128)(2,1)} %get-tuple-element.28), channel_id=1, source_target_pairs={{8,0},{16,8},{24,16},{32,24},{40,32},{48,40},{56,48},{64,56},{72,6... | collective-permute-start | bytes 393224 | tf_op jit(solution)/shard_map/ppermute | solution.py:20
  24.4 7.0 %copy-start.4 = (bf16[64,1,8,128]{3,0,2,1:T(8,128)(2,1)}, bf16[64,1,8,128]{3,0,2,1:T(8,128)(2,1)S(1)}, u32[]{:S(2)}) copy-start(bf16[64,1,8,128]{3,0,2,1:T(8,128)(2,1)S(1)} %collective-permute-done) | copy-start | bytes 393220
  24.4 8.2 %copy-start.6 = (bf16[64,1,8,128]{3,0,2,1:T(8,128)(2,1)}, bf16[64,1,8,128]{3,0,2,1:T(8,128)(2,1)S(1)}, u32[]{:S(2)}) copy-start(bf16[64,1,8,128]{3,0,2,1:T(8,128)(2,1)S(1)} %collective-permute-done.1) | copy-start | bytes 393220
  25.2 18.0 %collective-permute-start.2 = (bf16[64,10,1,128]{3,0,2,1:T(8,128)(2,1)}, bf16[64,10,1,128]{3,0,2,1:T(8,128)(2,1)}, u32[]{:S(2)}, u32[]{:S(2)}) collective-permute-start(bf16[64,10,1,128]{3,0,2,1:T(8,128)(2,1)} %get-tuple-element.23), channel_id=1, source_target_pairs={{0,1},{1,2},{2,3},{3,4},{4,5},{5,6},{6,7},{8,9},{9,10},{10,11},{11... | collective-permute-start | bytes 491528 | tf_op jit(solution)/shard_map/ppermute | solution.py:18
  31.4 11.9 %collective-permute-start.3 = (bf16[64,10,1,128]{3,0,2,1:T(8,128)(2,1)}, bf16[64,10,1,128]{3,0,2,1:T(8,128)(2,1)}, u32[]{:S(2)}, u32[]{:S(2)}) collective-permute-start(bf16[64,10,1,128]{3,0,2,1:T(8,128)(2,1)} %get-tuple-element.24), channel_id=1, source_target_pairs={{1,0},{2,1},{3,2},{4,3},{5,4},{6,5},{7,6},{9,8},{10,9},{11,10},{12... | collective-permute-start | bytes 491528 | tf_op jit(solution)/shard_map/ppermute | solution.py:20
  35.9 23.1 %collective-permute-start.6 = (bf16[64,10,1,128]{3,0,2,1:T(8,128)(2,1)S(1)}, bf16[64,10,1,128]{3,0,2,1:T(8,128)(2,1)S(1)}, u32[]{:S(2)}, u32[]{:S(2)}) collective-permute-start(bf16[64,10,1,128]{3,0,2,1:T(8,128)(2,1)S(1)} %get-tuple-element.21), channel_id=1, source_target_pairs={{0,1},{1,2},{2,3},{3,4},{4,5},{5,6},{6,7},{8,9},{9,10},{10,11},{11... | collective-permute-start | bytes 491528 | tf_op jit(solution)/shard_map/ppermute | solution.py:18
  41.4 17.6 %collective-permute-start.7 = (bf16[64,10,1,128]{3,0,2,1:T(8,128)(2,1)S(1)}, bf16[64,10,1,128]{3,0,2,1:T(8,128)(2,1)S(1)}, u32[]{:S(2)}, u32[]{:S(2)}) collective-permute-start(bf16[64,10,1,128]{3,0,2,1:T(8,128)(2,1)S(1)} %get-tuple-element.22), channel_id=1, source_target_pairs={{1,0},{2,1},{3,2},{4,3},{5,4},{6,5},{7,6},{9,8},{10,9},{11,10},{12... | collective-permute-start | bytes 491528 | tf_op jit(solution)/shard_map/ppermute | solution.py:20
  63.0 2.1 copy-start.10
  80.0 1.6 copy-start.3
  92.5 1.2 copy-start.9
  93.6 15.4 %collective-permute-start.8 = (bf16[64,1,8,128]{3,0,2,1:T(8,128)(2,1)S(1)}, bf16[64,1,8,128]{3,0,2,1:T(8,128)(2,1)S(1)}, u32[]{:S(2)}, u32[]{:S(2)}) collective-permute-start(bf16[64,1,8,128]{3,0,2,1:T(8,128)(2,1)S(1)} %get-tuple-element.25), channel_id=1, source_target_pairs={{0,8},{8,16},{16,24},{24,32},{32,40},{40,48},{48,56},{56,64},{64,7... | collective-permute-start | bytes 393224 | tf_op jit(solution)/shard_map/ppermute | solution.py:18
  98.1 10.9 %collective-permute-start.9 = (bf16[64,1,8,128]{3,0,2,1:T(8,128)(2,1)S(1)}, bf16[64,1,8,128]{3,0,2,1:T(8,128)(2,1)S(1)}, u32[]{:S(2)}, u32[]{:S(2)}) collective-permute-start(bf16[64,1,8,128]{3,0,2,1:T(8,128)(2,1)S(1)} %get-tuple-element.26), channel_id=1, source_target_pairs={{8,0},{16,8},{24,16},{32,24},{40,32},{48,40},{56,48},{64,56},{72,6... | collective-permute-start | bytes 393224 | tf_op jit(solution)/shard_map/ppermute | solution.py:20
  109.1 9.8 %collective-permute-start.10 = (bf16[64,10,1,128]{3,0,2,1:T(8,128)(2,1)S(1)}, bf16[64,10,1,128]{3,0,2,1:T(8,128)(2,1)S(1)}, u32[]{:S(2)}, u32[]{:S(2)}) collective-permute-start(bf16[64,10,1,128]{3,0,2,1:T(8,128)(2,1)S(1)} %get-tuple-element.19), channel_id=1, source_target_pairs={{0,1},{1,2},{2,3},{3,4},{4,5},{5,6},{6,7},{8,9},{9,10},{10,11},{11... | collective-permute-start | bytes 491528 | tf_op jit(solution)/shard_map/ppermute | solution.py:18
  114.9 7.6 %collective-permute-start.11 = (bf16[64,10,1,128]{3,0,2,1:T(8,128)(2,1)S(1)}, bf16[64,10,1,128]{3,0,2,1:T(8,128)(2,1)S(1)}, u32[]{:S(2)}, u32[]{:S(2)}) collective-permute-start(bf16[64,10,1,128]{3,0,2,1:T(8,128)(2,1)S(1)} %get-tuple-element.20), channel_id=1, source_target_pairs={{1,0},{2,1},{3,2},{4,3},{5,4},{6,5},{7,6},{9,8},{10,9},{11,10},{12... | collective-permute-start | bytes 491528 | tf_op jit(solution)/shard_map/ppermute | solution.py:20
  126.5 4.4 %copy-start.2 = (bf16[3,3,3,64,64]{4,3,2,1,0:T(8,128)(2,1)S(1)}, bf16[3,3,3,64,64]{4,3,2,1,0:T(8,128)(2,1)}, u32[]{:S(2)}) copy-start(bf16[3,3,3,64,64]{4,3,2,1,0:T(8,128)(2,1)} %copy.39) | copy-start | bytes 663556
  136.0 1.2 copy-start
  (2 other events, 1.9 us)
Sparse Core Ops, SparseCore 0:
  119.0 157.2 all-reduce.5
where the time goes:
time: 290 us; the launch traced here: 286 us
  waiting for transfers between devices  139 us (48%)
  matrix products  45.8 us (16%)
  starting transfers between devices  40.5 us (14%)
  other arithmetic  34.6 us (12%)
  between operations  14.9 us (5%)
  local copies, waits for them, and re-layouts  11.6 us (4%)
    psum x1, waiting for transfers between devices, shards(): summed_one, summed_two = lax.psum((partial_one, summed_two), ('gx', 'gy'))  135 us
    ppermute x6, starting transfers between devices, padded_2(): lax.ppermute(tail, axis, [(i, (i + 1) % count) for i in range(ends)])  30.2 us
    dot_general x27, matrix products, conv_pad(): jnp.einsum('co,cxyz->oxyz', folded[row_off, col_off], window, preferred_e...  26.6 us
    concatenate x3, other arithmetic, padded_2(): jnp.concatenate([lax.ppermute(tail, axis, [(i, (i + 1) % count) for i in...  11 us
    ppermute x6, starting transfers between devices, padded_2(): lax.ppermute(head, axis, [((i + 1) % count, i) for i in range(ends)])  10.3 us
    dot_general x9, matrix products, grad_forward(): jnp.einsum('cxyz,oxyz->co', window, grad, preferred_element_type=jnp.floa...  10 us
    dot_general x9, matrix products, grad_backward(): jnp.einsum('cxyz,kxyz->ck', activ, window, preferred_element_type=jnp.flo...  9.26 us
    concatenate x2, other arithmetic, stack_depth(): jnp.concatenate([padded[..., 0:depth], padded[..., 1:depth + 1], padded[....  9.24 us
  transfers between devices with their start and end apart: 13, of which 2 were waited for; matrix products, arithmetic and copies ran while one was open for 17% of the time, Pallas kernels for 0%

commit v1 on v0

--- a/solution.py
+++ b/solution.py
@@ -1,3 +1,4 @@
+import functools
 import math
 import jax
 import jax.numpy as jnp
@@ -5,6 +6,15 @@
 from jax.sharding import PartitionSpec as P
 
 BS = 8
+
+
+def slots_change(array_here, axis_key, which_axis):
+    for kk in (axis_key, which_axis):
+        array_here = lax.psum(array_here, axis_name=kk)
+    return array_here
+
+
+replace_chains_for = functools.partial(slots_change, axis_key="gy", which_axis="gx")
 
 
 def padded_2(cells, sides, width):
@@ -122,7 +132,7 @@
     partial_one = grad_forward(in_pad, pre_grad, tile_x, tile_y)
     branch = conv_pad(hidden_pad, flip_one, tile_x, tile_y)
     grad_features = (cell_f * (cotangent.astype(jnp.float32) + branch)).astype(jnp.bfloat16)
-    summed_one, summed_two = lax.psum((partial_one, summed_two), ("gx", "gy"))
+    summed_one, summed_two = replace_chains_for((partial_one, summed_two))
     return (grad_features, summed_one * scale, summed_two * scale)
 
 

time: 290 us -> 366 us (1.26)
  waiting for transfers between devices: 139 us -> 200 us
  matrix products: 45.8 us -> 61.4 us
    psum x1 -> x2, waiting for transfers between devices: 135 us -> 196 us  [slots_change(): array_here = lax.psum(array_here, axis_name=kk)]
    dot_general x27, matrix products: 26.6 us -> 42.1 us  [conv_pad(): jnp.einsum('co,cxyz->oxyz', folded[row_off, col_off], window, preferred_e...]
  transfers between devices with their start and end apart: 13 -> 14, of which waited for: 2 -> 3; matrix products, arithmetic and copies ran while one was open for 17% -> 18% of each run, Pallas kernels for 0% -> 0%
where the time goes in v1:
time: 366 us; the launch traced here: 362 us
  waiting for transfers between devices  200 us (55%)
  matrix products  61.4 us (17%)
  starting transfers between devices  40.4 us (11%)
  other arithmetic  34.7 us (9%)
  between operations  14.9 us (4%)
  local copies, waits for them, and re-layouts  11.1 us (3%)
    psum x2, waiting for transfers between devices, slots_change(): array_here = lax.psum(array_here, axis_name=kk)  196 us
    dot_general x27, matrix products, conv_pad(): jnp.einsum('co,cxyz->oxyz', folded[row_off, col_off], window, preferred_e...  42.1 us
    ppermute x6, starting transfers between devices, padded_2(): lax.ppermute(tail, axis, [(i, (i + 1) % count) for i in range(ends)])  30 us
    concatenate x3, other arithmetic, padded_2(): jnp.concatenate([lax.ppermute(tail, axis, [(i, (i + 1) % count) for i in...  11 us
    ppermute x6, starting transfers between devices, padded_2(): lax.ppermute(head, axis, [((i + 1) % count, i) for i in range(ends)])  10.1 us
    dot_general x9, matrix products, grad_forward(): jnp.einsum('cxyz,oxyz->co', window, grad, preferred_element_type=jnp.floa...  9.99 us
    concatenate x2, other arithmetic, stack_depth(): jnp.concatenate([padded[..., 0:depth], padded[..., 1:depth + 1], padded[....  9.26 us
    dot_general x9, matrix products, grad_backward(): jnp.einsum('cxyz,kxyz->ck', activ, window, preferred_element_type=jnp.flo...  9.26 us
  transfers between devices with their start and end apart: 14, of which 3 were waited for; matrix products, arithmetic and copies ran while one was open for 18% of the time, Pallas kernels for 0%

profile of v1, /device:TPU:1, one launch (start us, length us, event | category | flops | bytes accessed | tf_op | source)
XLA Modules:
  0.0 362.2 jit_solution(17886839819134775851)
XLA Ops:
  8.1 3.3 copy_multiply_fusion.1
  11.5 4.5 %collective-permute-start = (bf16[64,1,8,128]{3,0,2,1:T(8,128)(2,1)S(1)}, bf16[64,1,8,128]{3,0,2,1:T(8,128)(2,1)S(1)}, u32[]{:S(2)}, u32[]{:S(2)}) collective-permute-start(bf16[64,1,8,128]{3,0,2,1:T(8,128)(2,1)S(1)} %get-tuple-element.31), channel_id=1, source_target_pairs={{0,8},{8,16},{16,24},{24,32},{32,40},{40,48},{48,56},{56,64},{64,7... | collective-permute-start | bytes 393224 | tf_op jit(solution)/shard_map/ppermute | solution.py:28
  18.6 3.6 %collective-permute-start.4 = (bf16[64,1,8,128]{3,0,2,1:T(8,128)(2,1)}, bf16[64,1,8,128]{3,0,2,1:T(8,128)(2,1)S(1)}, u32[]{:S(2)}, u32[]{:S(2)}) collective-permute-start(bf16[64,1,8,128]{3,0,2,1:T(8,128)(2,1)} %get-tuple-element.29), channel_id=1, source_target_pairs={{0,8},{8,16},{16,24},{24,32},{32,40},{40,48},{48,56},{56,64},{64,7... | collective-permute-start | bytes 393224 | tf_op jit(solution)/shard_map/ppermute | solution.py:28
  25.1 6.2 %collective-permute-start.2 = (bf16[64,10,1,128]{3,0,2,1:T(8,128)(2,1)}, bf16[64,10,1,128]{3,0,2,1:T(8,128)(2,1)}, u32[]{:S(2)}, u32[]{:S(2)}) collective-permute-start(bf16[64,10,1,128]{3,0,2,1:T(8,128)(2,1)} %get-tuple-element.25), channel_id=1, source_target_pairs={{0,1},{1,2},{2,3},{3,4},{4,5},{5,6},{6,7},{8,9},{9,10},{10,11},{11... | collective-permute-start | bytes 491528 | tf_op jit(solution)/shard_map/ppermute | solution.py:28
  35.8 5.5 %collective-permute-start.6 = (bf16[64,10,1,128]{3,0,2,1:T(8,128)(2,1)S(1)}, bf16[64,10,1,128]{3,0,2,1:T(8,128)(2,1)S(1)}, u32[]{:S(2)}, u32[]{:S(2)}) collective-permute-start(bf16[64,10,1,128]{3,0,2,1:T(8,128)(2,1)S(1)} %get-tuple-element.23), channel_id=1, source_target_pairs={{0,1},{1,2},{2,3},{3,4},{4,5},{5,6},{6,7},{8,9},{9,10},{10,11},{11... | collective-permute-start | bytes 491528 | tf_op jit(solution)/shard_map/ppermute | solution.py:28
  43.1 4.0 %fusion.15 = bf16[64,10,10,130]{3,0,2,1:T(8,128)(2,1)S(1)} fusion(bf16[64,10,1,128]{3,0,2,1:T(8,128)(2,1)} %collective-permute-done.3, bf16[64,10,1,128]{3,0,2,1:T(8,128)(2,1)} %collective-permute-done.2, bf16[64,1,8,128]{3,0,2,1:T(8,128)(2,1)} %copy-done.7, bf16[64,8,8,128]{3,0,2,1:T(8,128)(2,1)S(1)} %get-tuple-element.34, bf16[64,1,8,128]{3,0,2,1:T(8,128)(2,1)} %copy-done.5), kind=kLoop, calls=%fused_computation.24 | loop fusion | flops 14976000 | bytes 3302400 | tf_op jit(solution)/shard_map/concatenate | solution.py:26
  48.1 4.9 %pad_maximum_fusion = bf16[192,10,10,128]{3,0,2,1:T(8,128)(2,1)S(1)} fusion(bf16[64,10,10,128]{3,0,2,1:T(8,128)(2,1)S(1)} %get-tuple-element.20, bf16[64,10,1,128]{3,0,2,1:T(8,128)(2,1)} %collective-permute-done.3, bf16[64,1,8,128]{3,0,2,1:T(8,128)(2,1)S(1)} %copy-done.8, bf16[64,8,8,128]{3,0,2,1:T(8,128)(2,1)S(1)} %get-tuple-element.34, ...), kind=kLoop, calls=%fused_computation.3 | loop fusion | flops 34406400 | bytes 9830400 | tf_op jit(solution)/shard_map/concatenate | solution.py:55
  59.0 3.9 %fusion.19 = bf16[64,10,10,130]{3,0,2,1:T(8,128)(2,1)S(1)} fusion(bf16[64,10,1,128]{3,0,2,1:T(8,128)(2,1)S(1)} %collective-permute-done.7, bf16[64,10,1,128]{3,0,2,1:T(8,128)(2,1)S(1)} %collective-permute-done.6, bf16[64,1,8,128]{3,0,2,1:T(8,128)(2,1)} %collective-permute-done.5, bf16[64,8,8,128]{3,0,2,1:T(8,128)(2,1)S(1)} %get-tuple-element.33, ...), kind=kLoop, calls=%fused_computation.28 | loop fusion | flops 14976000 | bytes 3302400 | tf_op jit(solution)/shard_map/concatenate | solution.py:26
  62.9 2.1 fusion.123
  66.8 5.5 %pad_maximum_fusion.4 = (bf16[192,10,10,128]{3,0,2,1:T(8,128)(2,1)S(1)}, bf16[192,10,10,128]{3,0,2,1:T(8,128)(2,1)S(1)}) fusion(bf16[64,10,10,128]{3,0,2,1:T(8,128)(2,1)S(1)} %get-tuple-element.17, bf16[64,10,10,128]{3,0,2,1:T(8,128)(2,1)} %get-tuple-element.18, bf16[64,10,1,128]{3,0,2,1:T(8,128)(2,1)S(1)} %collective-permute-done.7, ...), kind=kLoop, calls=%fused_computation.7 | loop fusion | flops 46694400 | bytes 14745600 | tf_op jit(solution)/shard_map/concatenate | solution.py:63
  86.8 2.1 fusion.76
  88.9 3.5 fusion.98
  93.6 4.5 %collective-permute-start.8 = (bf16[64,1,8,128]{3,0,2,1:T(8,128)(2,1)S(1)}, bf16[64,1,8,128]{3,0,2,1:T(8,128)(2,1)S(1)}, u32[]{:S(2)}, u32[]{:S(2)}) collective-permute-start(bf16[64,1,8,128]{3,0,2,1:T(8,128)(2,1)S(1)} %get-tuple-element.27), channel_id=1, source_target_pairs={{0,8},{8,16},{16,24},{24,32},{32,40},{40,48},{48,56},{56,64},{64,7... | collective-permute-start | bytes 393224 | tf_op jit(solution)/shard_map/ppermute | solution.py:28
  109.0 5.8 %collective-permute-start.10 = (bf16[64,10,1,128]{3,0,2,1:T(8,128)(2,1)S(1)}, bf16[64,10,1,128]{3,0,2,1:T(8,128)(2,1)S(1)}, u32[]{:S(2)}, u32[]{:S(2)}) collective-permute-start(bf16[64,10,1,128]{3,0,2,1:T(8,128)(2,1)S(1)} %get-tuple-element.21), channel_id=1, source_target_pairs={{0,1},{1,2},{2,3},{3,4},{4,5},{5,6},{6,7},{8,9},{9,10},{10,11},{11... | collective-permute-start | bytes 491528 | tf_op jit(solution)/shard_map/ppermute | solution.py:28
  118.9 3.5 collective-permute-done.11
  122.4 3.1 select_maximum_fusion
  126.4 4.4 %pad_maximum_fusion.3 = bf16[192,10,10,128]{3,0,2,1:T(8,128)(2,1)S(1)} fusion(bf16[64,10,10,128]{3,0,2,1:T(8,128)(2,1)S(1)} %get-tuple-element.16, bf16[64,10,1,128]{3,0,2,1:T(8,128)(2,1)S(1)} %collective-permute-done.11, bf16[64,1,8,128]{3,0,2,1:T(8,128)(2,1)S(1)} %collective-permute-done.9, bf16[64,8,8,128]{3,0,2,1:T(8,128)(2,1)S(1)} %fusion.98, ...), kind=kLoop, calls=%fused_computation.6 | loop fusion | flops 34406400 | bytes 9830400 | tf_op jit(solution)/shard_map/concatenate | solution.py:55
  131.5 2.1 fusion.46
  133.6 2.1 fusion.48
  137.8 2.2 fusion.52
  146.1 78.6 %all-reduce.10.cloned.1.call-done = (f32[3,3,3,64,64]{4,3,2,1,0:T(8,128)}, f32[3,3,3,64,64]{4,3,2,1,0:T(8,128)}) async-done(((f32[3,3,3,64,64]{4,3,2,1,0:T(8,128)}, f32[3,3,3,64,64]{4,3,2,1,0:T(8,128)}), (f32[3,3,3,64,64]{4,3,2,1,0:T(8,128)}, f32[3,3,3,64,64]{4,3,2,1,0:T(8,128)})) %all-reduce.10.cloned.1.call-update) | async-done | bytes 884752 | tf_op jit(solution)/shard_map/psum | solution.py:13
  224.7 8.4 %fusion.97 = bf16[64,8,8,128]{3,0,2,1:T(8,128)(2,1)S(1)} fusion(f32[8,8,128,64]{2,3,1,0:T(8,128)S(1)} %fusion.44, f32[8,8,128,64]{2,3,1,0:T(8,128)} %fusion.46, f32[8,8,128,64]{2,3,1,0:T(8,128)} %fusion.48, f32[8,8,128,64]{2,3,1,0:T(8,128)} %fusion.50, f32[8,8,128,64]{2,3,1,0:T(8,128)} %fusion.52, f32[8,8,128,64]{2,3,1,0:T(8,128)} %fusion.54, ...), kind=kOutput, calls=%fused_computation.107 | convolution fusion | flops 207618048 | bytes 22069760 | tf_op jit(solution)/shard_map/co,cxyz->oxyz/dot_general | solution.py:75
  234.8 117.5 %all-reduce.8.cloned.1.call-done = (f32[3,3,3,64,64]{4,3,2,1,0:T(8,128)}, f32[3,3,3,64,64]{4,3,2,1,0:T(8,128)}) async-done(((f32[3,3,3,64,64]{4,3,2,1,0:T(8,128)}, f32[3,3,3,64,64]{4,3,2,1,0:T(8,128)}), (f32[3,3,3,64,64]{4,3,2,1,0:T(8,128)}, f32[3,3,3,64,64]{4,3,2,1,0:T(8,128)})) %all-reduce.8.cloned.1.call-update) | async-done | bytes 884752 | tf_op jit(solution)/shard_map/psum | solution.py:13
  352.3 2.9 broadcast_multiply_fusion
  (118 shorter events, 63.2 us)
Async XLA Ops:
  7.2 217.5 %all-reduce.10.cloned.1.call-start = ((), (), s32[]{:S(2)}) async-start(), calls=%async_computation.1 | async-start | bytes 3538944 | tf_op jit(solution)/shard_map/psum | solution.py:13
  8.0 14.2 %copy-start.13 = (bf16[128]{0:T(256)(128)(2,1)}, bf16[128]{0:T(256)(128)(2,1)S(1)}, u32[]{:S(2)}) copy-start(bf16[128]{0:T(256)(128)(2,1)S(1)} %convert_element_type.40) | copy-start | bytes 772
  8.1 16.1 %copy-start.9 = (bf16[3,3,3,64,64]{4,3,2,1,0:T(8,128)(2,1)S(1)}, bf16[3,3,3,64,64]{4,3,2,1,0:T(8,128)(2,1)}, u32[]{:S(2)}) copy-start(bf16[3,3,3,64,64]{4,3,2,1,0:T(8,128)(2,1)} %param.9) | copy-start | bytes 663556
  8.1 24.5 %copy-start.2 = (bf16[3,3,3,64,64]{4,3,2,1,0:T(8,128)(2,1)S(1)}, bf16[3,3,3,64,64]{4,3,2,1,0:T(8,128)(2,1)}, u32[]{:S(2)}) copy-start(bf16[3,3,3,64,64]{4,3,2,1,0:T(8,128)(2,1)} %param.8) | copy-start | bytes 663556
  11.5 12.8 %collective-permute-start = (bf16[64,1,8,128]{3,0,2,1:T(8,128)(2,1)S(1)}, bf16[64,1,8,128]{3,0,2,1:T(8,128)(2,1)S(1)}, u32[]{:S(2)}, u32[]{:S(2)}) collective-permute-start(bf16[64,1,8,128]{3,0,2,1:T(8,128)(2,1)S(1)} %get-tuple-element.31), channel_id=1, source_target_pairs={{0,8},{8,16},{16,24},{24,32},{32,40},{40,48},{48,56},{56,64},{64,7... | collective-permute-start | bytes 393224 | tf_op jit(solution)/shard_map/ppermute | solution.py:28
  16.0 8.3 %collective-permute-start.1 = (bf16[64,1,8,128]{3,0,2,1:T(8,128)(2,1)S(1)}, bf16[64,1,8,128]{3,0,2,1:T(8,128)(2,1)S(1)}, u32[]{:S(2)}, u32[]{:S(2)}) collective-permute-start(bf16[64,1,8,128]{3,0,2,1:T(8,128)(2,1)S(1)} %get-tuple-element.32), channel_id=1, source_target_pairs={{8,0},{16,8},{24,16},{32,24},{40,32},{48,40},{56,48},{64,56},{72,6... | collective-permute-start | bytes 393224 | tf_op jit(solution)/shard_map/ppermute | solution.py:30
  18.6 16.4 %collective-permute-start.4 = (bf16[64,1,8,128]{3,0,2,1:T(8,128)(2,1)}, bf16[64,1,8,128]{3,0,2,1:T(8,128)(2,1)S(1)}, u32[]{:S(2)}, u32[]{:S(2)}) collective-permute-start(bf16[64,1,8,128]{3,0,2,1:T(8,128)(2,1)} %get-tuple-element.29), channel_id=1, source_target_pairs={{0,8},{8,16},{16,24},{24,32},{32,40},{40,48},{48,56},{56,64},{64,7... | collective-permute-start | bytes 393224 | tf_op jit(solution)/shard_map/ppermute | solution.py:28
  22.3 12.8 %collective-permute-start.5 = (bf16[64,1,8,128]{3,0,2,1:T(8,128)(2,1)}, bf16[64,1,8,128]{3,0,2,1:T(8,128)(2,1)}, u32[]{:S(2)}, u32[]{:S(2)}) collective-permute-start(bf16[64,1,8,128]{3,0,2,1:T(8,128)(2,1)} %get-tuple-element.30), channel_id=1, source_target_pairs={{8,0},{16,8},{24,16},{32,24},{40,32},{48,40},{56,48},{64,56},{72,6... | collective-permute-start | bytes 393224 | tf_op jit(solution)/shard_map/ppermute | solution.py:30
  24.2 8.4 %copy-start.14 = (bf16[128]{0:T(256)(128)(2,1)S(1)}, bf16[128]{0:T(256)(128)(2,1)}, u32[]{:S(2)}) copy-start(bf16[128]{0:T(256)(128)(2,1)} %copy-done.13) | copy-start | bytes 772
  24.3 7.0 %copy-start.5 = (bf16[64,1,8,128]{3,0,2,1:T(8,128)(2,1)}, bf16[64,1,8,128]{3,0,2,1:T(8,128)(2,1)S(1)}, u32[]{:S(2)}) copy-start(bf16[64,1,8,128]{3,0,2,1:T(8,128)(2,1)S(1)} %collective-permute-done) | copy-start | bytes 393220
  24.3 6.9 %copy-start.7 = (bf16[64,1,8,128]{3,0,2,1:T(8,128)(2,1)}, bf16[64,1,8,128]{3,0,2,1:T(8,128)(2,1)S(1)}, u32[]{:S(2)}) copy-start(bf16[64,1,8,128]{3,0,2,1:T(8,128)(2,1)S(1)} %collective-permute-done.1) | copy-start | bytes 393220
  25.1 18.0 %collective-permute-start.2 = (bf16[64,10,1,128]{3,0,2,1:T(8,128)(2,1)}, bf16[64,10,1,128]{3,0,2,1:T(8,128)(2,1)}, u32[]{:S(2)}, u32[]{:S(2)}) collective-permute-start(bf16[64,10,1,128]{3,0,2,1:T(8,128)(2,1)} %get-tuple-element.25), channel_id=1, source_target_pairs={{0,1},{1,2},{2,3},{3,4},{4,5},{5,6},{6,7},{8,9},{9,10},{10,11},{11... | collective-permute-start | bytes 491528 | tf_op jit(solution)/shard_map/ppermute | solution.py:28
  31.2 11.9 %collective-permute-start.3 = (bf16[64,10,1,128]{3,0,2,1:T(8,128)(2,1)}, bf16[64,10,1,128]{3,0,2,1:T(8,128)(2,1)}, u32[]{:S(2)}, u32[]{:S(2)}) collective-permute-start(bf16[64,10,1,128]{3,0,2,1:T(8,128)(2,1)} %get-tuple-element.26), channel_id=1, source_target_pairs={{1,0},{2,1},{3,2},{4,3},{5,4},{6,5},{7,6},{9,8},{10,9},{11,10},{12... | collective-permute-start | bytes 491528 | tf_op jit(solution)/shard_map/ppermute | solution.py:30
  35.8 23.1 %collective-permute-start.6 = (bf16[64,10,1,128]{3,0,2,1:T(8,128)(2,1)S(1)}, bf16[64,10,1,128]{3,0,2,1:T(8,128)(2,1)S(1)}, u32[]{:S(2)}, u32[]{:S(2)}) collective-permute-start(bf16[64,10,1,128]{3,0,2,1:T(8,128)(2,1)S(1)} %get-tuple-element.23), channel_id=1, source_target_pairs={{0,1},{1,2},{2,3},{3,4},{4,5},{5,6},{6,7},{8,9},{9,10},{10,11},{11... | collective-permute-start | bytes 491528 | tf_op jit(solution)/shard_map/ppermute | solution.py:28
  41.3 17.6 %collective-permute-start.7 = (bf16[64,10,1,128]{3,0,2,1:T(8,128)(2,1)S(1)}, bf16[64,10,1,128]{3,0,2,1:T(8,128)(2,1)S(1)}, u32[]{:S(2)}, u32[]{:S(2)}) collective-permute-start(bf16[64,10,1,128]{3,0,2,1:T(8,128)(2,1)S(1)} %get-tuple-element.24), channel_id=1, source_target_pairs={{1,0},{2,1},{3,2},{4,3},{5,4},{6,5},{7,6},{9,8},{10,9},{11,10},{12... | collective-permute-start | bytes 491528 | tf_op jit(solution)/shard_map/ppermute | solution.py:30
  93.6 15.4 %collective-permute-start.8 = (bf16[64,1,8,128]{3,0,2,1:T(8,128)(2,1)S(1)}, bf16[64,1,8,128]{3,0,2,1:T(8,128)(2,1)S(1)}, u32[]{:S(2)}, u32[]{:S(2)}) collective-permute-start(bf16[64,1,8,128]{3,0,2,1:T(8,128)(2,1)S(1)} %get-tuple-element.27), channel_id=1, source_target_pairs={{0,8},{8,16},{16,24},{24,32},{32,40},{40,48},{48,56},{56,64},{64,7... | collective-permute-start | bytes 393224 | tf_op jit(solution)/shard_map/ppermute | solution.py:28
  98.0 10.9 %collective-permute-start.9 = (bf16[64,1,8,128]{3,0,2,1:T(8,128)(2,1)S(1)}, bf16[64,1,8,128]{3,0,2,1:T(8,128)(2,1)S(1)}, u32[]{:S(2)}, u32[]{:S(2)}) collective-permute-start(bf16[64,1,8,128]{3,0,2,1:T(8,128)(2,1)S(1)} %get-tuple-element.28), channel_id=1, source_target_pairs={{8,0},{16,8},{24,16},{32,24},{40,32},{48,40},{56,48},{64,56},{72,6... | collective-permute-start | bytes 393224 | tf_op jit(solution)/shard_map/ppermute | solution.py:30
  109.0 9.8 %collective-permute-start.10 = (bf16[64,10,1,128]{3,0,2,1:T(8,128)(2,1)S(1)}, bf16[64,10,1,128]{3,0,2,1:T(8,128)(2,1)S(1)}, u32[]{:S(2)}, u32[]{:S(2)}) collective-permute-start(bf16[64,10,1,128]{3,0,2,1:T(8,128)(2,1)S(1)} %get-tuple-element.21), channel_id=1, source_target_pairs={{0,1},{1,2},{2,3},{3,4},{4,5},{5,6},{6,7},{8,9},{9,10},{10,11},{11... | collective-permute-start | bytes 491528 | tf_op jit(solution)/shard_map/ppermute | solution.py:28
  114.8 7.6 %collective-permute-start.11 = (bf16[64,10,1,128]{3,0,2,1:T(8,128)(2,1)S(1)}, bf16[64,10,1,128]{3,0,2,1:T(8,128)(2,1)S(1)}, u32[]{:S(2)}, u32[]{:S(2)}) collective-permute-start(bf16[64,10,1,128]{3,0,2,1:T(8,128)(2,1)S(1)} %get-tuple-element.22), channel_id=1, source_target_pairs={{1,0},{2,1},{3,2},{4,3},{5,4},{6,5},{7,6},{9,8},{10,9},{11,10},{12... | collective-permute-start | bytes 491528 | tf_op jit(solution)/shard_map/ppermute | solution.py:30
  118.6 233.7 %all-reduce.8.cloned.1.call-start = ((), (), s32[]{:S(2)}) async-start(), calls=%async_computation | async-start | bytes 3538944 | tf_op jit(solution)/shard_map/psum | solution.py:13
  126.4 4.4 %copy-start.3 = (bf16[3,3,3,64,64]{4,3,2,1,0:T(8,128)(2,1)S(1)}, bf16[3,3,3,64,64]{4,3,2,1,0:T(8,128)(2,1)}, u32[]{:S(2)}) copy-start(bf16[3,3,3,64,64]{4,3,2,1,0:T(8,128)(2,1)} %copy.39) | copy-start | bytes 663556
  130.8 13.3 %copy-start = (bf16[192,10,10,128]{3,0,2,1:T(8,128)(2,1)}, bf16[192,10,10,128]{3,0,2,1:T(8,128)(2,1)S(1)}, u32[]{:S(2)}) copy-start(bf16[192,10,10,128]{3,0,2,1:T(8,128)(2,1)S(1)} %pad_maximum_fusion.3) | copy-start | bytes 14745604
  144.1 80.7 %copy-start.1 = (bf16[64,8,8,128]{3,2,1,0:T(8,128)(2,1)S(1)}, bf16[64,8,8,128]{3,2,1,0:T(8,128)(2,1)}, u32[]{:S(2)}) copy-start(bf16[64,8,8,128]{3,2,1,0:T(8,128)(2,1)} %param.6) | copy-start | bytes 3145732
  144.1 80.7 %copy-start.12 = (f32[128]{0:T(128)S(1)}, f32[128]{0:T(128)}, u32[]{:S(2)}) copy-start(f32[128]{0:T(128)} %convert_element_type.41) | copy-start | bytes 1540
  (5 other events, 6.8 us)
Sparse Core Ops, SparseCore 0:
  118.7 105.8 all-reduce.9
  227.3 124.9 all-reduce.7
